TPU v7x, 256 devices: a whole 4x4x8 slice. The times are simulated.
256 devices in a mesh: gx: 8 (over x, core), gy: 4 (over y), gz: 8 (over z).
Axes of the slice: x: 4, y: 4, z: 8, core: 2. Of those that a mesh axis runs over, the one named last changes fastest.
Arguments:
- blocks: bfloat16 [4096, 128, 1024], P(('gx', 'gy', 'gz')), may hold values from -0.375 to 0.375
- counts: int32 [4096], P(('gx', 'gy', 'gz')), may hold values from 1 to 128
- owner: int32 [4096, 1], P(('gx', 'gy', 'gz')), may hold values from 0 to 31; in each aligned block of 16 rows (0 to 15, 16 to 31, ...) no two rows name the same one
- kdiag: float32 [256, 1024], P(('gx', 'gy', 'gz')), may hold values from 0.5 to 4
- rhs: float32 [256, 1024], P(('gx', 'gy', 'gz')), may hold values from -40 to 40
- modes: float32 [256, 6, 1024], P(('gx', 'gy', 'gz')), may hold values from -6 to 6
Outputs:
- schur: bfloat16 [256, 1024, 1024], P(('gx', 'gy', 'gz'))
- solution: float32 [256, 1024], P(('gx', 'gy', 'gz'))
- residual: float32 [256, 1024], P(('gx', 'gy', 'gz'))
Inputs may be any that keep to these rules, and one draw needn't show every extreme that they name: `owner`: the 16 blocks of one device go to different owners.
All inputs are finite; a program needn't handle non-finite values.
Results may differ from a plain program's by a relative error of at most 0.001.
Values may be sent and summed in bfloat16 or wider, within the bound.
No kernel may reach another device: no remote copies, remote signals or barrier semaphores. Data moves between devices by JAX's collectives and lax.ppermute only.
A program may use at most 64 MiB of HBM per device.

v0:
```python
import functools

import jax
import jax.numpy as jnp
from jax import lax
from jax.sharding import Mesh
from jax.sharding import PartitionSpec as P

ITERS = 2
GX_GY_GZ = ("gx_0", "gx_1", "gy", "gz")
GX = ("gx_0", "gx_1")


def with_halo(array, sides, width):
    edges = {}
    for axis, dim in sides:
        devices, length = (lax.axis_size(axis), array.shape[dim])
        up = [(i, (i + 1) % devices) for i in range(devices)]
        last = lax.slice_in_dim(array, length - width, length, axis=dim)
        initial = lax.slice_in_dim(array, 0, width, axis=dim)
        edges[dim] = (
            lax.ppermute(last, axis, up),
            lax.ppermute(initial, axis, [(b, a) for a, b in up]),
        )
    done = []
    for _, dim in sides:
        low, high = edges[dim]
        around = [(width, width) if d in done else (0, 0) for d in range(array.ndim)]
        array = jnp.concatenate([jnp.pad(low, around), array, jnp.pad(high, around)], axis=dim)
        done.append(dim)
    return array


def by_axis(array, axes):
    return functools.reduce(lax.psum, axes, array)


def add_faces(values, grid):
    width = values.shape[1]
    face = width // 8
    extra = jnp.concatenate(
        [
            grid[2, 1, 1][:, face : 2 * face],
            grid[0, 1, 1][:, 0:face],
            grid[1, 2, 1][:, 3 * face : 4 * face],
            grid[1, 0, 1][:, 2 * face : 3 * face],
            grid[1, 1, 2][:, 6 * face : 8 * face],
            grid[1, 1, 0][:, 4 * face : 6 * face],
        ],
        axis=1,
    )
    return values + extra


def shards(blocks, counts, owner, kdiag, rhs, modes):
    hi = lax.Precision.HIGHEST
    nblk, nrows, width = blocks.shape
    size_y = lax.axis_size("gy")
    size_z = lax.axis_size("gz")
    owners = size_y * size_z
    rowid = lax.broadcasted_iota(jnp.int32, (nblk, nrows, 1), 1)
    masked = jnp.where(rowid < counts[:, None, None], blocks, jnp.zeros_like(blocks))
    target = lax.broadcasted_iota(jnp.int32, (owners, nblk), 0)
    pick = (owner[:, 0][None, :] == target).astype(jnp.bfloat16)
    outgoing = jnp.dot(
        pick, masked.reshape(nblk, nrows * width), preferred_element_type=jnp.bfloat16
    )
    outgoing = outgoing.reshape(owners, nrows, width)
    arrived = lax.all_to_all(outgoing, ("gy", "gz"), split_axis=0, concat_axis=0, tiled=True)
    flat = arrived.reshape(owners * nrows, width)
    gram = lax.dot_general(flat, flat, (((0,), (0,)), ((), ())), preferred_element_type=jnp.float32)
    stiff = gram + jnp.diag(kdiag[0])
    schur = stiff.astype(jnp.bfloat16)[None]
    stacked = jnp.concatenate([rhs, modes[0]], axis=0)
    grid = with_halo(stacked[None, None, None], ((GX, 0), ("gy", 1), ("gz", 2)), 1)
    loaded = add_faces(stacked, grid)
    force = loaded[0]
    basis = loaded[1:]
    coarse, gforce, fnorm = (
        by_axis(0.5 * jnp.dot(basis, basis.T, precision=hi), GX_GY_GZ),
        by_axis(0.5 * jnp.dot(basis, force, precision=hi), GX_GY_GZ),
        by_axis(0.5 * jnp.sum(force * force), GX_GY_GZ),
    )
    factor = jnp.linalg.cholesky(coarse)
    coef = jax.scipy.linalg.cho_solve((factor, True), gforce)
    residual = force - jnp.dot(coef, basis, precision=hi)
    norm_now = fnorm - jnp.dot(gforce, coef, precision=hi)
    direction = residual
    solution = jnp.zeros_like(force)
    for step in range(ITERS):
        local = jnp.dot(stiff, direction, precision=hi)
        faces = with_halo(local[None, None, None, None], ((GX, 0), ("gy", 1), ("gz", 2)), 1)
        image = add_faces(local[None], faces)[0]
        gimage, curve, square, cross = (
            by_axis(0.5 * jnp.dot(basis, image, precision=hi), GX_GY_GZ),
            by_axis(0.5 * jnp.sum(direction * image), GX_GY_GZ),
            by_axis(0.5 * jnp.sum(image * image), GX_GY_GZ),
            by_axis(0.5 * jnp.sum(residual * image), GX_GY_GZ),
        )
        coef = jax.scipy.linalg.cho_solve((factor, True), gimage)
        along = image - jnp.dot(coef, basis, precision=hi)
        alpha = norm_now / curve
        along_sq = (
            square
            - 2.0 * jnp.dot(coef, gimage, precision=hi)
            + jnp.dot(coef, jnp.dot(coarse, coef, precision=hi), precision=hi)
        )
        norm_next = norm_now - 2.0 * alpha * cross + alpha * alpha * along_sq
        solution = solution + alpha * direction
        residual = residual - alpha * along
        direction = residual + norm_next / norm_now * direction
        norm_now = norm_next
    return (schur, solution[None], residual[None])


def solution(mesh):
    split = Mesh(
        mesh.devices.reshape(4, 2, mesh.shape["gy"], mesh.shape["gz"]), ("gx_0", "gx_1", "gy", "gz")
    )
    in_specs = (
        P(GX_GY_GZ, None, None),
        P(GX_GY_GZ),
        P(GX_GY_GZ, None),
        P(GX_GY_GZ, None),
        P(GX_GY_GZ, None),
        P(GX_GY_GZ, None, None),
    )
    out_specs = (P(GX_GY_GZ, None, None), P(GX_GY_GZ, None), P(GX_GY_GZ, None))
    return jax.shard_map(
        shards, mesh=split, in_specs=in_specs, out_specs=out_specs, check_vma=False
    )
```

profile of v0, /device:TPU:32, one launch (start us, length us, event | category | flops | bytes accessed | tf_op | source)
XLA Modules:
  0.0 398.1 jit_solution(9656893630817966385)
XLA Ops:
  0.6 0.7 iota_compare_fusion.2
  1.4 2.5 broadcast_select_fusion
  3.9 4.8 %fusion = bf16[32,128,1024]{2,0,1:T(8,128)(2,1)} fusion(s32[16]{0:T(128)S(1)} %bitcast.242, bf16[2,8,128,1024]{3,2,1,0:T(8,128)(2,1)S(1)} %bitcast.205), kind=kOutput, calls=%fused_computation | convolution fusion | flops 134218240 | bytes 12582976 | tf_op jit(solution)/shard_map/dot_general | solution.py:65
  8.6 11.3 %copy.15 = bf16[32,128,1024]{2,1,0:T(8,128)(2,1)} copy(bf16[32,128,1024]{2,0,1:T(8,128)(2,1)} %fusion) | data formatting | bytes 16777216 | tf_op jit(solution)/shard_map/dot_general | solution.py:65
  20.0 11.5 %all-to-all-start = ((bf16[32,128,1024]{2,1,0:T(8,128)(2,1)}), bf16[32,128,1024]{2,1,0:T(8,128)(2,1)}, u32[]{:S(2)}, u32[]{:S(2)}) async-start(bf16[32,128,1024]{2,1,0:T(8,128)(2,1)} %copy.15), calls=%async_computation | async-start | bytes 16777216 | tf_op jit(solution)/shard_map/all_to_all | solution.py:69
  31.6 1.6 collective-permute-start
  33.2 2.7 collective-permute-start.2
  36.5 1.5 collective-permute-start.5
  38.0 12.2 %collective-permute-done.2 = f32[1,1,1,7,1024]{4,3,2,1,0:T(8,128)S(1)} collective-permute-done((f32[1,1,1,7,1024]{4,3,2,1,0:T(8,128)S(1)}, f32[1,1,1,7,1024]{4,3,2,1,0:T(8,128)S(1)}, u32[]{:S(2)}, u32[]{:S(2)}) %collective-permute-start.2) | collective-permute-done | bytes 28704 | tf_op jit(solution)/shard_map/ppermute | solution.py:23
  50.2 2.1 collective-permute-done.3
  52.3 163.7 %collective-permute-done.4 = f32[1,1,1,7,1024]{4,3,2,1,0:T(8,128)S(1)} collective-permute-done((f32[1,1,1,7,1024]{4,3,2,1,0:T(8,128)S(1)}, f32[1,1,1,7,1024]{4,3,2,1,0:T(8,128)S(1)}, u32[]{:S(2)}, u32[]{:S(2)}) %collective-permute-start.4) | collective-permute-done | bytes 28704 | tf_op jit(solution)/shard_map/ppermute | solution.py:23
  216.1 5.7 %collective-permute-done.5 = f32[1,1,1,7,1024]{4,3,2,1,0:T(8,128)S(1)} collective-permute-done((f32[1,1,1,7,1024]{4,3,2,1,0:T(8,128)S(1)}, f32[1,1,1,7,1024]{4,3,2,1,0:T(8,128)S(1)}, u32[]{:S(2)}, u32[]{:S(2)}) %collective-permute-start.5) | collective-permute-done | bytes 28704 | tf_op jit(solution)/shard_map/ppermute | solution.py:22
  222.2 10.5 %all-reduce.8 = (f32[6,6]{1,0:T(8,128)S(1)}, f32[6]{0:T(128)S(1)}) all-reduce(f32[6,6]{1,0:T(8,128)S(1)} %convolution_multiply_fusion, f32[6]{0:T(128)S(1)} %fusion.13), channel_id=1, replica_groups=mesh['gx_0'=4,'gx_1'=2,'gy'=4,'gz'=8] {'gx_0'}, use_global_device_ids=true, to_apply=%region_9.10 | all-reduce | flops 42 | bytes 336 | tf_op jit(solution)/shard_map/psum | solution.py:35
  232.7 2.5 all-reduce.11
  235.2 7.8 %all-reduce.5 = (f32[6,6]{1,0:T(8,128)S(1)}, f32[6]{0:T(128)S(1)}) all-reduce(f32[6,6]{1,0:T(8,128)S(1)} %get-tuple-element.36, f32[6]{0:T(128)S(1)} %get-tuple-element.37), channel_id=1, replica_groups=mesh['gx_0'=4,'gx_1'=2,'gy'=4,'gz'=8] {'gy'}, use_global_device_ids=true, to_apply=%region_11.12 | all-reduce | flops 42 | bytes 336 | tf_op jit(solution)/shard_map/psum | solution.py:35
  243.0 16.3 %all-reduce.2 = (f32[6,6]{1,0:T(8,128)S(1)}, f32[6]{0:T(128)S(1)}) all-reduce(f32[6,6]{1,0:T(8,128)S(1)} %get-tuple-element.20, f32[6]{0:T(128)S(1)} %get-tuple-element.21), channel_id=1, replica_groups=mesh['gx_0'=4,'gx_1'=2,'gy'=4,'gz'=8] {'gz'}, use_global_device_ids=true, to_apply=%region_12.13 | all-reduce | flops 42 | bytes 336 | tf_op jit(solution)/shard_map/psum | solution.py:35
  260.0 0.6 compare_reduce_fusion
  260.7 0.6 fusion.31
  261.9 0.8 fusion.48
  262.8 0.6 multiply_reduce_fusion.3
  263.4 13.1 %fusion.53 = f32[1024,1024,1]{1,0,2:T(8,128)S(1)} fusion(bf16[32,128,1024]{2,1,0:T(8,128)(2,1)} %all-to-all-done), kind=kOutput, calls=%fused_computation.111 | convolution fusion | flops 8589934592 | bytes 12582912 | tf_op jit(solution)/shard_map/dot_general | solution.py:71
  276.5 1.9 copy-done
  278.5 3.7 fusion.4
  283.9 1.5 collective-permute-start.9
  285.4 2.5 collective-permute-start.10
  287.9 1.3 collective-permute-done.10
  289.2 2.3 collective-permute-done.11
  291.5 0.6 multiply_reduce_fusion.1
  293.6 9.6 %all-reduce.7 = (f32[]{:T(128)}, f32[]{:T(128)}, f32[]{:T(128)}, f32[6]{0:T(128)S(1)}) all-reduce(f32[]{:T(128)S(6)} %mul.83, f32[]{:T(128)S(6)} %mul.88, f32[]{:T(128)S(6)} %mul.95, f32[6]{0:T(128)S(1)} %fusion.12), channel_id=1, replica_groups=mesh['gx_0'=4,'gx_1'=2,'gy'=4,'gz'=8] {'gx_0'}, use_global_device_ids=true, to_apply=%region_1.2 | all-reduce | flops 9 | bytes 72 | tf_op jit(solution)/shard_map/psum | solution.py:35
  303.2 3.1 all-reduce.10
  306.3 9.6 %all-reduce.4 = (f32[]{:T(128)}, f32[]{:T(128)}, f32[]{:T(128)}, f32[6]{0:T(128)S(1)}) all-reduce(f32[]{:T(128)} %get-tuple-element.32, f32[]{:T(128)} %get-tuple-element.33, f32[]{:T(128)} %get-tuple-element.34, f32[6]{0:T(128)S(1)} %get-tuple-element.35), channel_id=1, replica_groups=mesh['gx_0'=4,'gx_1'=2,'gy'=4,'gz'=8] {'gy'}, use_global_device_ids=true, to_apply=%region_3.4 | all-reduce | flops 9 | bytes 72 | tf_op jit(solution)/shard_map/psum | solution.py:35
  315.9 16.2 %all-reduce.1 = (f32[]{:T(128)}, f32[]{:T(128)}, f32[]{:T(128)}, f32[6]{0:T(128)S(1)}) all-reduce(f32[]{:T(128)} %get-tuple-element.16, f32[]{:T(128)} %get-tuple-element.17, f32[]{:T(128)} %get-tuple-element.18, f32[6]{0:T(128)S(1)} %get-tuple-element.19), channel_id=1, replica_groups=mesh['gx_0'=4,'gx_1'=2,'gy'=4,'gz'=8] {'gz'}, use_global_device_ids=true, to_apply=%region_4.5 | all-reduce | flops 9 | bytes 72 | tf_op jit(solution)/shard_map/psum | solution.py:35
  332.2 0.8 fusion.45
  333.1 0.8 fusion.15
  338.6 5.9 %fusion.3 = f32[1,1024]{1,0:T(1,128)S(1)} fusion(f32[1024,1]{0,1:T(1,128)S(1)} %bitcast.209, f32[1024,1024,1]{1,0,2:T(8,128)} %copy-done, f32[1024]{0:T(1024)S(1)} %bitcast.215), kind=kOutput, calls=%fused_computation.6 | convolution fusion | flops 15728640 | bytes 4206592 | tf_op jit(solution)/shard_map/dot_general | solution.py:91
  345.0 0.8 collective-permute-start.14
  345.8 1.2 collective-permute-start.15
  347.0 0.8 collective-permute-start.16
  347.8 1.2 collective-permute-start.17
  349.1 1.5 collective-permute-done.16
  350.6 0.8 collective-permute-done.17
  351.5 0.6 multiply_reduce_fusion
  352.9 4.0 fusion.6
  356.9 9.5 %all-reduce.6 = (f32[]{:T(128)}, f32[6]{0:T(128)S(1)}) all-reduce(f32[]{:T(128)S(6)} %mul.103, f32[6]{0:T(128)S(1)} %fusion.11), channel_id=1, replica_groups=mesh['gx_0'=4,'gx_1'=2,'gy'=4,'gz'=8] {'gx_0'}, use_global_device_ids=true, to_apply=%region_30.32 | all-reduce | flops 7 | bytes 56 | tf_op jit(solution)/shard_map/psum | solution.py:35
  366.3 3.1 all-reduce.9
  369.4 9.8 %all-reduce.3 = (f32[]{:T(128)}, f32[6]{0:T(128)S(1)}) all-reduce(f32[]{:T(128)} %get-tuple-element.30, f32[6]{0:T(128)S(1)} %get-tuple-element.31), channel_id=1, replica_groups=mesh['gx_0'=4,'gx_1'=2,'gy'=4,'gz'=8] {'gy'}, use_global_device_ids=true, to_apply=%region_32.34 | all-reduce | flops 7 | bytes 56 | tf_op jit(solution)/shard_map/psum | solution.py:35
  379.2 17.2 %all-reduce = (f32[]{:T(128)}, f32[6]{0:T(128)S(1)}) all-reduce(f32[]{:T(128)} %get-tuple-element.14, f32[6]{0:T(128)S(1)} %get-tuple-element.15), channel_id=1, replica_groups=mesh['gx_0'=4,'gx_1'=2,'gy'=4,'gz'=8] {'gz'}, use_global_device_ids=true, to_apply=%region_33.35 | all-reduce | flops 7 | bytes 56 | tf_op jit(solution)/shard_map/psum | solution.py:35
  397.5 0.6 multiply_subtract_fusion
  (74 shorter events, 5.2 us)
Async XLA Ops:
  1.4 2.5 copy-start.4
  19.9 11.6 %copy-start.2 = (f32[1,6,1024]{2,0,1:T(1,128)S(1)}, f32[1,6,1024]{2,0,1:T(1,128)}, u32[]{:S(2)}) copy-start(f32[1,6,1024]{2,0,1:T(1,128)} %param.13) | copy-start | bytes 73732
  19.9 11.6 %copy-start.3 = (f32[1,1024]{1,0:T(1,128)S(1)}, f32[1,1024]{1,0:T(1,128)}, u32[]{:S(2)}) copy-start(f32[1,1024]{1,0:T(1,128)} %param.12) | copy-start | bytes 12292
  20.0 243.5 %all-to-all-start = ((bf16[32,128,1024]{2,1,0:T(8,128)(2,1)}), bf16[32,128,1024]{2,1,0:T(8,128)(2,1)}, u32[]{:S(2)}, u32[]{:S(2)}) async-start(bf16[32,128,1024]{2,1,0:T(8,128)(2,1)} %copy.15), calls=%async_computation | async-start | bytes 16777216 | tf_op jit(solution)/shard_map/all_to_all | solution.py:69
  31.6 4.9 %collective-permute-start = (f32[1,1,1,7,1024]{4,3,2,1,0:T(8,128)S(1)}, f32[1,1,1,7,1024]{4,3,2,1,0:T(8,128)S(1)}, u32[]{:S(2)}, u32[]{:S(2)}) collective-permute-start(f32[1,1,1,7,1024]{4,3,2,1,0:T(8,128)S(1)} %fusion.17), channel_id=1, source_target_pairs={{32,0},{64,32},{96,64},{128,96},{160,128},{192,160},{224,192},{0,2... | collective-permute-start | bytes 86024 | tf_op jit(solution)/shard_map/ppermute | solution.py:23
  33.2 4.8 %collective-permute-start.1 = (f32[1,1,1,7,1024]{4,3,2,1,0:T(8,128)S(1)}, f32[1,1,1,7,1024]{4,3,2,1,0:T(8,128)S(1)}, u32[]{:S(2)}, u32[]{:S(2)}) collective-permute-start(f32[1,1,1,7,1024]{4,3,2,1,0:T(8,128)S(1)} %fusion.17), channel_id=1, source_target_pairs={{0,32},{32,64},{64,96},{96,128},{128,160},{160,192},{192,224},{224... | collective-permute-start | bytes 86024 | tf_op jit(solution)/shard_map/ppermute | solution.py:22
  33.2 17.0 %collective-permute-start.2 = (f32[1,1,1,7,1024]{4,3,2,1,0:T(8,128)S(1)}, f32[1,1,1,7,1024]{4,3,2,1,0:T(8,128)S(1)}, u32[]{:S(2)}, u32[]{:S(2)}) collective-permute-start(f32[1,1,1,7,1024]{4,3,2,1,0:T(8,128)S(1)} %fusion.17), channel_id=1, source_target_pairs={{8,0},{16,8},{24,16},{0,24},{9,1},{17,9},{25,17},{1,25},{10,2},{18... | collective-permute-start | bytes 86024 | tf_op jit(solution)/shard_map/ppermute | solution.py:23
  35.9 16.4 %collective-permute-start.3 = (f32[1,1,1,7,1024]{4,3,2,1,0:T(8,128)S(1)}, f32[1,1,1,7,1024]{4,3,2,1,0:T(8,128)S(1)}, u32[]{:S(2)}, u32[]{:S(2)}) collective-permute-start(f32[1,1,1,7,1024]{4,3,2,1,0:T(8,128)S(1)} %fusion.17), channel_id=1, source_target_pairs={{0,8},{8,16},{16,24},{24,0},{1,9},{9,17},{17,25},{25,1},{2,10},{10... | collective-permute-start | bytes 86024 | tf_op jit(solution)/shard_map/ppermute | solution.py:22
  35.9 180.1 %collective-permute-start.4 = (f32[1,1,1,7,1024]{4,3,2,1,0:T(8,128)S(1)}, f32[1,1,1,7,1024]{4,3,2,1,0:T(8,128)S(1)}, u32[]{:S(2)}, u32[]{:S(2)}) collective-permute-start(f32[1,1,1,7,1024]{4,3,2,1,0:T(8,128)S(1)} %fusion.17), channel_id=1, source_target_pairs={{1,0},{2,1},{3,2},{4,3},{5,4},{6,5},{7,6},{0,7},{9,8},{10,9},{11,1... | collective-permute-start | bytes 86024 | tf_op jit(solution)/shard_map/ppermute | solution.py:23
  36.5 185.3 %collective-permute-start.5 = (f32[1,1,1,7,1024]{4,3,2,1,0:T(8,128)S(1)}, f32[1,1,1,7,1024]{4,3,2,1,0:T(8,128)S(1)}, u32[]{:S(2)}, u32[]{:S(2)}) collective-permute-start(f32[1,1,1,7,1024]{4,3,2,1,0:T(8,128)S(1)} %fusion.17), channel_id=1, source_target_pairs={{0,1},{1,2},{2,3},{3,4},{4,5},{5,6},{6,7},{7,0},{8,9},{9,10},{10,1... | collective-permute-start | bytes 86024 | tf_op jit(solution)/shard_map/ppermute | solution.py:22
  263.4 15.0 %copy-start.1 = (f32[1,1024]{1,0:T(1,128)S(1)}, f32[1,1024]{1,0:T(1,128)}, u32[]{:S(2)}) copy-start(f32[1,1024]{1,0:T(1,128)} %param.11) | copy-start | bytes 12292
  276.5 1.9 copy-start
  282.2 5.7 %collective-permute-start.6 = (f32[1,1,1,1,1024]{4,3,2,1,0:T(1,128)S(1)}, f32[1,1,1,1,1024]{4,3,2,1,0:T(1,128)S(1)}, u32[]{:S(2)}, u32[]{:S(2)}) collective-permute-start(f32[1,1,1,1,1024]{4,3,2,1,0:T(1,128)S(1)} %bitcast.217), channel_id=1, source_target_pairs={{32,0},{64,32},{96,64},{128,96},{160,128},{192,160},{224,192},{0,2... | collective-permute-start | bytes 12296 | tf_op jit(solution)/shard_map/ppermute | solution.py:23
  282.8 5.0 %collective-permute-start.7 = (f32[1,1,1,1,1024]{4,3,2,1,0:T(1,128)S(1)}, f32[1,1,1,1,1024]{4,3,2,1,0:T(1,128)S(1)}, u32[]{:S(2)}, u32[]{:S(2)}) collective-permute-start(f32[1,1,1,1,1024]{4,3,2,1,0:T(1,128)S(1)} %bitcast.218), channel_id=1, source_target_pairs={{0,32},{32,64},{64,96},{96,128},{128,160},{160,192},{192,224},{224... | collective-permute-start | bytes 12296 | tf_op jit(solution)/shard_map/ppermute | solution.py:22
  283.4 4.6 %collective-permute-start.8 = (f32[1,1,1,1,1024]{4,3,2,1,0:T(1,128)S(1)}, f32[1,1,1,1,1024]{4,3,2,1,0:T(1,128)S(1)}, u32[]{:S(2)}, u32[]{:S(2)}) collective-permute-start(f32[1,1,1,1,1024]{4,3,2,1,0:T(1,128)S(1)} %bitcast.219), channel_id=1, source_target_pairs={{8,0},{16,8},{24,16},{0,24},{9,1},{17,9},{25,17},{1,25},{10,2},{18... | collective-permute-start | bytes 12296 | tf_op jit(solution)/shard_map/ppermute | solution.py:23
  283.9 7.6 %collective-permute-start.9 = (f32[1,1,1,1,1024]{4,3,2,1,0:T(1,128)S(1)}, f32[1,1,1,1,1024]{4,3,2,1,0:T(1,128)S(1)}, u32[]{:S(2)}, u32[]{:S(2)}) collective-permute-start(f32[1,1,1,1,1024]{4,3,2,1,0:T(1,128)S(1)} %bitcast.220), channel_id=1, source_target_pairs={{0,8},{8,16},{16,24},{24,0},{1,9},{9,17},{17,25},{25,1},{2,10},{10... | collective-permute-start | bytes 12296 | tf_op jit(solution)/shard_map/ppermute | solution.py:22
  285.4 3.8 collective-permute-start.10
  287.9 3.6 collective-permute-start.11
  344.4 3.4 collective-permute-start.12
  344.4 4.6 %collective-permute-start.13 = (f32[1,1,1,1,1024]{4,3,2,1,0:T(1,128)S(1)}, f32[1,1,1,1,1024]{4,3,2,1,0:T(1,128)S(1)}, u32[]{:S(2)}, u32[]{:S(2)}) collective-permute-start(f32[1,1,1,1,1024]{4,3,2,1,0:T(1,128)S(1)} %bitcast.225), channel_id=1, source_target_pairs={{0,32},{32,64},{64,96},{96,128},{128,160},{160,192},{192,224},{224... | collective-permute-start | bytes 12296 | tf_op jit(solution)/shard_map/ppermute | solution.py:22
  345.0 4.1 %collective-permute-start.14 = (f32[1,1,1,1,1024]{4,3,2,1,0:T(1,128)S(1)}, f32[1,1,1,1,1024]{4,3,2,1,0:T(1,128)S(1)}, u32[]{:S(2)}, u32[]{:S(2)}) collective-permute-start(f32[1,1,1,1,1024]{4,3,2,1,0:T(1,128)S(1)} %bitcast.226), channel_id=1, source_target_pairs={{8,0},{16,8},{24,16},{0,24},{9,1},{17,9},{25,17},{1,25},{10,2},{18... | collective-permute-start | bytes 12296 | tf_op jit(solution)/shard_map/ppermute | solution.py:23
  345.8 5.6 %collective-permute-start.15 = (f32[1,1,1,1,1024]{4,3,2,1,0:T(1,128)S(1)}, f32[1,1,1,1,1024]{4,3,2,1,0:T(1,128)S(1)}, u32[]{:S(2)}, u32[]{:S(2)}) collective-permute-start(f32[1,1,1,1,1024]{4,3,2,1,0:T(1,128)S(1)} %bitcast.227), channel_id=1, source_target_pairs={{0,8},{8,16},{16,24},{24,0},{1,9},{9,17},{17,25},{25,1},{2,10},{10... | collective-permute-start | bytes 12296 | tf_op jit(solution)/shard_map/ppermute | solution.py:22
  347.0 3.6 collective-permute-start.16
  347.8 3.6 collective-permute-start.17
where the time goes:
time: 399 us; the launch traced here: 398 us
  waiting for transfers between devices  190 us (48%)
  blocking collectives  115 us (29%)
  matrix products  31.4 us (8%)
  starting transfers between devices  27.6 us (7%)
  local copies, waits for them, and re-layouts  13.4 us (3%)
  other arithmetic  12 us (3%)
  between operations  8.86 us (2%)
    ppermute x9, waiting for transfers between devices, with_halo(): lax.ppermute(initial, axis, [(b, a) for a, b in up])  179 us
    psum x12, blocking collectives, by_axis(): return functools.reduce(lax.psum, axes, array)  115 us
    dot_general x1, matrix products, shards(): lax.dot_general(flat, flat, (((0,), (0,)), ((), ())), preferred_element_t...  13.1 us
    all_to_all x1, starting transfers between devices, shards(): lax.all_to_all(outgoing, ('gy', 'gz'), split_axis=0, concat_axis=0, tiled...  11.5 us
    dot_general x1, local copies, waits for them, and re-layouts, shards(): jnp.dot(pick, masked.reshape(nblk, nrows * width), preferred_element_type...  11.3 us
    ppermute x9, waiting for transfers between devices, with_halo(): lax.ppermute(last, axis, up)  11 us
    ppermute x9, starting transfers between devices, with_halo(): lax.ppermute(initial, axis, [(b, a) for a, b in up])  9.65 us
    dot_general x2, matrix products, shards(): local = jnp.dot(stiff, direction, precision=hi)  9.54 us
  transfers between devices with their start and end apart: 19, of which 8 were waited for; matrix products, arithmetic and copies ran while one was open for 1% of the time, Pallas kernels for 0%

commit v1 on v0

v1 whole, which is shorter than its diff:
```python
import functools

import jax
import jax.numpy as jnp
from jax import lax
from jax.experimental import pallas as pl
from jax.experimental.pallas import tpu as pltpu
from jax.sharding import Mesh
from jax.sharding import PartitionSpec as P

GX_GY_GZ = ("gx_0", "gx_1", "gy", "gz")
GX = ("gx_0", "gx_1")
HI = lax.Precision.HIGHEST
CUTS = (96, 32)
STEP = 4


def ring(axis, shift):
    n = lax.axis_size(axis)
    return [(i, (i + shift) % n) for i in range(n)]


def assembled(values):
    f = values.shape[1] // 8
    spans = ((0, f), (f, 2 * f), (2 * f, 3 * f), (3 * f, 4 * f), (4 * f, 6 * f), (6 * f, 8 * f))
    extra = []
    for axis, (plus, minus) in zip((GX, "gy", "gz"), (spans[0:2], spans[2:4], spans[4:6])):
        extra.append(lax.ppermute(values[:, minus[0] : minus[1]], axis, ring(axis, -1)))
        extra.append(lax.ppermute(values[:, plus[0] : plus[1]], axis, ring(axis, 1)))
    return values + jnp.concatenate(extra, axis=1)


def pack_body(cuts, slot, live, *refs):
    step = pl.program_id(0)
    ins, outs = refs[:STEP], refs[STEP:]
    nrows, width = ins[0].shape[1:]
    rows = lax.broadcasted_iota(jnp.int32, (nrows, width), 0)
    for k in range(STEP):
        x = ins[k][0]
        x = jnp.where(rows < live[step * STEP + k], x, jnp.zeros_like(x))
        start = 0
        for out, size in zip(outs, cuts):
            out[k] = x[start : start + size]
            start += size


def pack(blocks, counts, owner, owners):
    nblk, nrows, width = blocks.shape
    hit = owner[:, 0][None, :] == lax.broadcasted_iota(jnp.int32, (owners, nblk), 0)
    slot = jnp.sum(jnp.where(hit, jnp.arange(nblk, dtype=jnp.int32)[None, :], 0), axis=1)
    live = jnp.sum(jnp.where(hit, counts[None, :], 0), axis=1)

    def source(k):
        return lambda i, slot, live: (slot[i * STEP + k], 0, 0)

    return pl.pallas_call(
        functools.partial(pack_body, CUTS),
        grid_spec=pltpu.PrefetchScalarGridSpec(
            num_scalar_prefetch=2,
            grid=(owners // STEP,),
            in_specs=[pl.BlockSpec((1, nrows, width), source(k)) for k in range(STEP)],
            out_specs=[pl.BlockSpec((STEP, c, width), lambda i, *_: (i, 0, 0)) for c in CUTS],
        ),
        out_shape=[jax.ShapeDtypeStruct((owners, c, width), blocks.dtype) for c in CUTS],
        name="pack",
    )(slot, live, *([blocks] * STEP))


def everyone(tile, axes):
    n = 1
    for axis in axes:
        n *= lax.axis_size(axis)
    copies = jnp.broadcast_to(tile[None], (n, *tile.shape))
    return jnp.sum(lax.all_to_all(copies, axes, 0, 0, tiled=True), axis=0)


def coefficients(g, nv):
    row = lax.broadcasted_iota(jnp.int32, g.shape, 0)
    col = lax.broadcasted_iota(jnp.int32, g.shape, 1)
    e = g
    for j in range(1, nv):
        pivot = jnp.sum(jnp.where(row == j, e, 0.0), axis=0, keepdims=True)
        column = jnp.sum(jnp.where(col == j, e, 0.0), axis=1, keepdims=True)
        corner = jnp.sum(jnp.where(col[:1] == j, pivot, 0.0), axis=1, keepdims=True)
        scaled = pivot / corner
        e = jnp.where(row == j, scaled, jnp.where(row == 0, e, e - column * scaled))
    e = jnp.where(row == 0, 0.0, e)

    def part(a, k):
        return a[:, k * nv : (k + 1) * nv]

    r8 = lax.broadcasted_iota(jnp.int32, (g.shape[0], nv), 0)
    c8 = lax.broadcasted_iota(jnp.int32, (g.shape[0], nv), 1)

    def as_row(v):
        return jnp.sum(jnp.where(r8 == c8, v, 0.0), axis=0, keepdims=True)

    def times(a, v_row):
        return jnp.sum(a * v_row, axis=1, keepdims=True)

    def dot(u, v):
        return jnp.sum(u * v, axis=0, keepdims=True)

    ga, gb, gc, gd = (part(g, k) for k in range(4))
    ib, ic = part(e, 1), part(e, 2)
    c0 = e[:, 0:1]
    first = jnp.where(r8[:, :1] == 0, 1.0, 0.0)
    q = first - c0
    rr = ga[0:1, 0:1] - dot(ga[:, 0:1] * (1.0 - first), c0)
    qr = as_row(q)
    p1 = times(ib, qr)
    p1r = as_row(p1)
    gbq, gaq = times(gb, qr), times(ga, qr)
    curve = dot(q, gbq) - dot(p1, gaq)
    alpha = rr / curve
    a = q + alpha * p1
    b = -alpha * q
    ar, br = qr + alpha * p1r, -alpha * qr
    gcb = times(gc, br)
    rr1 = dot(a, times(ga, ar)) + 2.0 * dot(a, times(gb, br)) + dot(b, gcb)
    beta = rr1 / rr
    d = a + beta * q
    dr = ar + beta * qr
    p2 = times(ib, dr) + times(ic, br)
    curve2 = (
        dot(d, times(gb, dr))
        + 2.0 * dot(d, gcb)
        + dot(b, times(gd, br))
        - dot(p2, times(ga, dr))
        - dot(p2, times(gb, br))
    )
    alpha2 = rr1 / curve2
    sol = (alpha * q + alpha2 * d, alpha2 * b)
    res = (a + alpha2 * p2, b - alpha2 * d, -alpha2 * b)
    return sol, res


def finish_body(nv, parts_ref, x_ref, w_ref, z_ref, sol_ref, res_ref):
    g = parts_ref[0]
    for i in range(1, parts_ref.shape[0]):
        g = g + parts_ref[i]
    sol, res = coefficients(g, nv)
    x, w, z = x_ref[...], w_ref[...], z_ref[...]
    sol_ref[...] = jnp.sum(sol[0][:nv] * x + sol[1][:nv] * w, axis=0, keepdims=True)
    res_ref[...] = jnp.sum(res[0][:nv] * x + res[1][:nv] * w + res[2][:nv] * z, axis=0, keepdims=True)


def shards(blocks, counts, owner, kdiag, rhs, modes):
    width = blocks.shape[2]
    owners = lax.axis_size("gy") * lax.axis_size("gz")
    x = assembled(jnp.concatenate([rhs, modes[0]], axis=0))
    nv = x.shape[0]
    stiff = jnp.diag(kdiag[0])
    for outgoing in pack(blocks, counts, owner, owners):
        arrived = lax.all_to_all(outgoing, ("gy", "gz"), split_axis=0, concat_axis=0, tiled=True)
        flat = arrived.reshape(-1, width)
        stiff = stiff + lax.dot_general(
            flat, flat, (((0,), (0,)), ((), ())), preferred_element_type=jnp.float32
        )
    schur = stiff.astype(jnp.bfloat16)[None]
    v1 = jnp.dot(x, stiff, precision=HI)
    w = assembled(v1)
    v2 = jnp.dot(w, stiff, precision=HI)
    near = jnp.dot(x, 0.5 * jnp.concatenate([x, w], axis=0).T, precision=HI)
    far = jnp.dot(w, jnp.concatenate([0.5 * w, v2], axis=0).T, precision=HI)
    mine = jnp.concatenate([near, far], axis=1)
    mine = jnp.pad(mine, ((0, 8 - nv), (0, 128 - 4 * nv)))
    z = assembled(v2)
    some = everyone(mine, ("gy", "gz"))
    gx = lax.axis_size(GX)
    parts = lax.all_to_all(jnp.broadcast_to(some[None], (gx, 8, 128)), GX, 0, 0, tiled=True)
    sol, res = pl.pallas_call(
        functools.partial(finish_body, nv),
        out_shape=[jax.ShapeDtypeStruct((1, width), jnp.float32)] * 2,
        name="finish",
    )(parts, x, w, z)
    return (schur, sol, res)


def solution(mesh):
    split = Mesh(mesh.devices.reshape(4, 2, mesh.shape["gy"], mesh.shape["gz"]), GX_GY_GZ)
    in_specs = (
        P(GX_GY_GZ, None, None),
        P(GX_GY_GZ),
        P(GX_GY_GZ, None),
        P(GX_GY_GZ, None),
        P(GX_GY_GZ, None),
        P(GX_GY_GZ, None, None),
    )
    out_specs = (P(GX_GY_GZ, None, None), P(GX_GY_GZ, None), P(GX_GY_GZ, None))
    return jax.shard_map(
        shards, mesh=split, in_specs=in_specs, out_specs=out_specs, check_vma=False
    )
```

time: 399 us -> 286 us (0.72)
  waiting for transfers between devices: 190 us -> 50.4 us
  blocking collectives: 115 us -> 152 us
  starting transfers between devices: 27.6 us -> 41.4 us
  Pallas kernels: 0 us -> 12.7 us
  local copies, waits for them, and re-layouts: 13.4 us -> 1.97 us
  matrix products: 31.4 us -> 21.1 us
  other arithmetic: 12 us -> 3.68 us
  between operations: 8.86 us -> 0.83 us
    all_to_all x0 -> x1, blocking collectives: none -> 152 us  [shards(): lax.all_to_all(outgoing, ('gy', 'gz'), split_axis=0, concat_axis=0, tiled...]
    ppermute x18, waiting for transfers between devices: 190 us -> 43.5 us  [the longest x9 35.5 us: assembled(): lax.ppermute(values[:, minus[0]:minus[1]], axis, ring(axis, -1))]
    psum x12 -> x0, blocking collectives: 115 us -> none  [by_axis(): return functools.reduce(lax.psum, axes, array)]
    all_to_all x0 -> x2, starting transfers between devices: none -> 15 us  [the longest x1 11.7 us: everyone(): return jnp.sum(lax.all_to_all(copies, axes, 0, 0, tiled=True), axis=0)]
    pallas_call x0 -> x2, Pallas kernels: none -> 12.7 us  [the longest x1 9.68 us: pack(): pl.pallas_call(functools.partial(pack_body, CUTS), grid_spec=pltpu.Prefet...]
    dot_general x11 -> x4, matrix products: 16.2 us -> 4.48 us  [the longest x1 2.08 us: shards(): v2 = jnp.dot(w, stiff, precision=HI)]
    dot_general x1 -> x0, local copies, waits for them, and re-layouts: 11.3 us -> none  [shards(): jnp.dot(pick, masked.reshape(nblk, nrows * width), preferred_element_type...]
    all_to_all x0 -> x2, waiting for transfers between devices: none -> 6.86 us  [the longest x1 4.74 us: shards(): lax.all_to_all(jnp.broadcast_to(some[None], (gx, 8, 128)), GX, 0, 0, tile...]
  transfers between devices with their start and end apart: 19 -> 21, of which waited for: 8 -> 8; matrix products, arithmetic and copies ran while one was open for 1% -> 5% of each run, Pallas kernels for 0% -> 0%
where the time goes in v1:
time: 286 us; the launch traced here: 284 us
  blocking collectives  152 us (53%)
  waiting for transfers between devices  50.4 us (18%)
  starting transfers between devices  41.4 us (14%)
  matrix products  21.1 us (7%)
  Pallas kernels  12.7 us (4%)
  other arithmetic  3.68 us (1%)
    all_to_all x1, blocking collectives, shards(): lax.all_to_all(outgoing, ('gy', 'gz'), split_axis=0, concat_axis=0, tiled...  152 us
    ppermute x9, waiting for transfers between devices, assembled(): lax.ppermute(values[:, minus[0]:minus[1]], axis, ring(axis, -1))  35.5 us
    ppermute x9, starting transfers between devices, assembled(): lax.ppermute(values[:, minus[0]:minus[1]], axis, ring(axis, -1))  17.7 us
    dot_general x2, matrix products, shards(): lax.dot_general(flat, flat, (((0,), (0,)), ((), ())), preferred_element_t...  16.7 us
    all_to_all x1, starting transfers between devices, everyone(): return jnp.sum(lax.all_to_all(copies, axes, 0, 0, tiled=True), axis=0)  11.7 us
    pallas_call x1, Pallas kernels, pack(): pl.pallas_call(functools.partial(pack_body, CUTS), grid_spec=pltpu.Prefet...  9.68 us
    ppermute x9, waiting for transfers between devices, assembled(): extra.append(lax.ppermute(values[:, plus[0]:plus[1]], axis, ring(axis, 1)))  8.02 us
  transfers between devices with their start and end apart: 21, of which 8 were waited for; matrix products, arithmetic and copies ran while one was open for 5% of the time, Pallas kernels for 0%

profile of v1, /device:TPU:32, one launch (start us, length us, event | category | flops | bytes accessed | tf_op | source)
XLA Modules:
  0.0 283.7 jit_solution(5826945224037940128)
XLA Ops:
  0.6 1.3 select_reduce_fusion
  1.9 9.7 %pack.1 = (bf16[32,96,1024]{2,1,0:T(8,128)(2,1)}, bf16[32,32,1024]{2,1,0:T(8,128)(2,1)}) custom-call(s32[32]{0:T(128)} %get-tuple-element.12.slot, s32[32]{0:T(128)} %get-tuple-element.11.live, bf16[16,128,1024]{2,1,0:T(8,128)(2,1)} %refs_3_.1, bf16[16,128,1024]{2,1,0:T(8,128)(2,1)} %refs_3_.1, bf16[16,128,1024]{2,1,0:T(8,128)(2,1)} %refs_3_.1, ...), custom_call_target="tpu_custom_call" | custom-call | tf_op jit(solution)/shard_map/pack/pallas_call | solution.py:56
  11.6 151.7 %all_to_all.20 = bf16[32,96,1024]{2,1,0:T(8,128)(2,1)} all-to-all(bf16[32,96,1024]{2,1,0:T(8,128)(2,1)} %get-tuple-element.7), channel_id=1, replica_groups=mesh['gx_0'=4,'gx_1'=2,'gy'=4,'gz'=8] {'gy','gz'}, dimensions={0} | all-to-all | bytes 12582912 | tf_op jit(solution)/shard_map/all_to_all | solution.py:155
  163.3 5.3 %all-to-all-start.1 = ((bf16[32,32,1024]{2,1,0:T(8,128)(2,1)}), bf16[32,32,1024]{2,1,0:T(8,128)(2,1)S(1)}, u32[]{:S(2)}, u32[]{:S(2)}) async-start(bf16[32,32,1024]{2,1,0:T(8,128)(2,1)} %get-tuple-element.8), calls=%async_computation.1 | async-start | bytes 4194304 | tf_op jit(solution)/shard_map/all_to_all | solution.py:155
  168.6 2.1 collective-permute-start
  170.7 0.0 collective-permute-start.1
  170.7 2.7 collective-permute-start.2
  173.5 0.6 collective-permute-start.4
  174.1 1.5 collective-permute-start.5
  175.6 0.7 collective-permute-done.2
  176.3 2.0 collective-permute-done.3
  178.3 34.7 %collective-permute-done.4 = f32[7,256]{1,0:T(8,128)S(1)} collective-permute-done((f32[7,256]{1,0:T(8,128)S(1)}, f32[7,256]{1,0:T(8,128)S(1)}, u32[]{:S(2)}, u32[]{:S(2)}) %collective-permute-start.4) | collective-permute-done | bytes 7200 | tf_op jit(solution)/shard_map/ppermute | solution.py:28
  213.0 0.0 copy-start.5
  213.1 12.1 %fusion.22 = f32[1024,1024,1]{1,0,2:T(8,128)} fusion(bf16[32,96,1024]{2,1,0:T(8,128)(2,1)} %all_to_all.20), kind=kOutput, calls=%fused_computation.66 | convolution fusion | flops 6442450944 | bytes 10485760 | tf_op jit(solution)/shard_map/dot_general | solution.py:157
  225.2 0.0 all-to-all-done.1
  225.2 4.6 %bitcast_add_fusion = f32[1024,1024]{1,0:T(8,128)S(1)} fusion(f32[1024,1024,1]{1,0,2:T(8,128)} %fusion.22, bf16[32,32,1024]{2,1,0:T(8,128)(2,1)S(1)} %all-to-all-done.1, f32[1024]{0:T(1024)S(1)} %bitcast.27), kind=kOutput, calls=%fused_computation | convolution fusion | flops 2151677952 | bytes 10489856 | tf_op jit(solution)/shard_map/dot_general | solution.py:157
  229.7 1.7 convert_bitcast_fusion
  231.4 2.1 fusion.23
  233.5 2.5 collective-permute-start.6
  236.0 2.9 %collective-permute-start.8 = (f32[7,128]{1,0:T(8,128)S(1)}, f32[7,128]{1,0:T(8,128)S(1)}, u32[]{:S(2)}, u32[]{:S(2)}) collective-permute-start(f32[7,128]{1,0:T(8,128)S(1)} %get-tuple-element.30), channel_id=1, source_target_pairs={{0,24},{8,0},{16,8},{24,16},{1,25},{9,1},{17,9},{25,17},{2,26},{10... | collective-permute-start | bytes 10760 | tf_op jit(solution)/shard_map/ppermute | solution.py:28
  238.9 0.0 collective-permute-start.9
  238.9 2.2 collective-permute-start.10
  241.1 0.0 collective-permute-done.6
  241.1 0.4 collective-permute-start.11
  241.5 2.2 collective-permute-done.9
  243.7 0.0 collective-permute-done.10
  243.7 1.0 collective-permute-done.11
  244.8 2.1 fusion.24
  246.8 0.2 fusion
  247.0 0.2 fusion.3
  247.2 1.3 collective-permute-start.12
  248.5 0.1 select_maximum_fusion
  248.6 0.7 broadcast_in_dim.62
  249.2 11.7 %all-to-all-start.2 = ((f32[32,8,128]{2,1,0:T(8,128)}), f32[32,8,128]{2,1,0:T(8,128)S(1)}, u32[]{:S(2)}, u32[]{:S(2)}) async-start(f32[32,8,128]{2,1,0:T(8,128)} %broadcast_in_dim.62), calls=%async_computation.2 | async-start | bytes 262144 | tf_op jit(solution)/shard_map/all_to_all | solution.py:74
  260.9 0.0 collective-permute-start.13
  260.9 2.8 collective-permute-start.14
  263.8 0.0 collective-permute-start.15
  263.8 0.6 collective-permute-start.16
  264.3 1.5 collective-permute-start.17
  265.8 0.0 collective-permute-done.14
  265.8 2.8 collective-permute-done.15
  268.6 2.1 all-to-all-done.2
  270.8 0.6 broadcast_in_dim.63
  271.4 3.3 %all-to-all-start.3 = ((f32[8,8,128]{2,1,0:T(8,128)}), f32[8,8,128]{2,1,0:T(8,128)S(1)}, u32[]{:S(2)}, u32[]{:S(2)}) async-start(f32[8,8,128]{2,1,0:T(8,128)} %broadcast_in_dim.63), calls=%async_computation.3 | async-start | bytes 65536 | tf_op jit(solution)/shard_map/all_to_all | solution.py:171
  274.8 0.6 add.21.z_ref
  275.4 4.7 %all-to-all-done.3.parts_ref = f32[8,8,128]{2,1,0:T(8,128)S(1)} async-done(((f32[8,8,128]{2,1,0:T(8,128)}), f32[8,8,128]{2,1,0:T(8,128)S(1)}, u32[]{:S(2)}, u32[]{:S(2)}) %all-to-all-start.3) | async-done | bytes 32800 | tf_op jit(solution)/shard_map/all_to_all | solution.py:171
  280.1 0.6 copy-done.2
  280.7 3.0 %finish.1 = (f32[1,1024]{1,0:T(1,128)}, f32[1,1024]{1,0:T(1,128)}) custom-call(f32[8,8,128]{2,1,0:T(8,128)} %copy-done.2, f32[7,1024]{1,0:T(8,128)} %copy-done.1, f32[7,1024]{1,0:T(8,128)} %copy-done, f32[7,1024]{1,0:T(8,128)} %add.21.z_ref), custom_call_target="tpu_custom_call" | custom-call | tf_op jit(solution)/shard_map/finish/pallas_call | solution.py:172
  (49 shorter events, 0.2 us)
Async XLA Ops:
  163.2 5.3 %copy-start.4 = (f32[1,6,1024]{2,0,1:T(1,128)S(1)}, f32[1,6,1024]{2,0,1:T(1,128)}, u32[]{:S(2)}) copy-start(f32[1,6,1024]{2,0,1:T(1,128)} %param.11) | copy-start | bytes 73732
  163.2 5.4 %copy-start.3 = (f32[1,1024]{1,0:T(1,128)S(1)}, f32[1,1024]{1,0:T(1,128)}, u32[]{:S(2)}) copy-start(f32[1,1024]{1,0:T(1,128)} %param.10) | copy-start | bytes 12292
  163.3 61.9 %all-to-all-start.1 = ((bf16[32,32,1024]{2,1,0:T(8,128)(2,1)}), bf16[32,32,1024]{2,1,0:T(8,128)(2,1)S(1)}, u32[]{:S(2)}, u32[]{:S(2)}) async-start(bf16[32,32,1024]{2,1,0:T(8,128)(2,1)} %get-tuple-element.8), calls=%async_computation.1 | async-start | bytes 4194304 | tf_op jit(solution)/shard_map/all_to_all | solution.py:155
  168.6 5.5 %collective-permute-start = (f32[7,128]{1,0:T(8,128)S(1)}, f32[7,128]{1,0:T(8,128)S(1)}, u32[]{:S(2)}, u32[]{:S(2)}) collective-permute-start(f32[7,128]{1,0:T(8,128)S(1)} %get-tuple-element.18), channel_id=1, source_target_pairs={{0,224},{32,0},{64,32},{96,64},{128,96},{160,128},{192,160},{224,1... | collective-permute-start | bytes 10760 | tf_op jit(solution)/shard_map/ppermute | solution.py:28
  170.7 4.9 %collective-permute-start.1 = (f32[7,128]{1,0:T(8,128)S(1)}, f32[7,128]{1,0:T(8,128)S(1)}, u32[]{:S(2)}, u32[]{:S(2)}) collective-permute-start(f32[7,128]{1,0:T(8,128)S(1)} %get-tuple-element.19), channel_id=1, source_target_pairs={{0,32},{32,64},{64,96},{96,128},{128,160},{160,192},{192,224},{224... | collective-permute-start | bytes 10760 | tf_op jit(solution)/shard_map/ppermute | solution.py:29
  170.7 5.6 %collective-permute-start.2 = (f32[7,128]{1,0:T(8,128)S(1)}, f32[7,128]{1,0:T(8,128)S(1)}, u32[]{:S(2)}, u32[]{:S(2)}) collective-permute-start(f32[7,128]{1,0:T(8,128)S(1)} %get-tuple-element.20), channel_id=1, source_target_pairs={{0,24},{8,0},{16,8},{24,16},{1,25},{9,1},{17,9},{25,17},{2,26},{10... | collective-permute-start | bytes 10760 | tf_op jit(solution)/shard_map/ppermute | solution.py:28
  173.5 4.8 %collective-permute-start.3 = (f32[7,128]{1,0:T(8,128)S(1)}, f32[7,128]{1,0:T(8,128)S(1)}, u32[]{:S(2)}, u32[]{:S(2)}) collective-permute-start(f32[7,128]{1,0:T(8,128)S(1)} %get-tuple-element.17), channel_id=1, source_target_pairs={{0,8},{8,16},{16,24},{24,0},{1,9},{9,17},{17,25},{25,1},{2,10},{10... | collective-permute-start | bytes 10760 | tf_op jit(solution)/shard_map/ppermute | solution.py:29
  173.5 39.5 %collective-permute-start.4 = (f32[7,256]{1,0:T(8,128)S(1)}, f32[7,256]{1,0:T(8,128)S(1)}, u32[]{:S(2)}, u32[]{:S(2)}) collective-permute-start(f32[7,256]{1,0:T(8,128)S(1)} %get-tuple-element.16), channel_id=1, source_target_pairs={{0,7},{1,0},{2,1},{3,2},{4,3},{5,4},{6,5},{7,6},{8,15},{9,8},{10,9... | collective-permute-start | bytes 21512 | tf_op jit(solution)/shard_map/ppermute | solution.py:28
  174.1 38.9 %collective-permute-start.5 = (f32[7,256]{1,0:T(8,128)S(1)}, f32[7,256]{1,0:T(8,128)S(1)}, u32[]{:S(2)}, u32[]{:S(2)}) collective-permute-start(f32[7,256]{1,0:T(8,128)S(1)} %get-tuple-element.15), channel_id=1, source_target_pairs={{0,1},{1,2},{2,3},{3,4},{4,5},{5,6},{6,7},{7,0},{8,9},{9,10},{10,1... | collective-permute-start | bytes 21512 | tf_op jit(solution)/shard_map/ppermute | solution.py:29
  213.0 33.8 %copy-start.1 = (f32[7,1024]{1,0:T(8,128)}, f32[7,1024]{1,0:T(8,128)S(1)}, u32[]{:S(2)}) copy-start(f32[7,1024]{1,0:T(8,128)S(1)} %fusion.7.x_ref) | copy-start | bytes 86020
  213.0 12.1 %copy-start.5 = (f32[1,1024]{1,0:T(1,128)S(1)}, f32[1,1024]{1,0:T(1,128)}, u32[]{:S(2)}) copy-start(f32[1,1024]{1,0:T(1,128)} %param.9) | copy-start | bytes 12292
  233.5 7.6 %collective-permute-start.6 = (f32[7,128]{1,0:T(8,128)S(1)}, f32[7,128]{1,0:T(8,128)S(1)}, u32[]{:S(2)}, u32[]{:S(2)}) collective-permute-start(f32[7,128]{1,0:T(8,128)S(1)} %get-tuple-element.32), channel_id=1, source_target_pairs={{0,224},{32,0},{64,32},{96,64},{128,96},{160,128},{192,160},{224,1... | collective-permute-start | bytes 10760 | tf_op jit(solution)/shard_map/ppermute | solution.py:28
  236.0 5.5 %collective-permute-start.7 = (f32[7,128]{1,0:T(8,128)S(1)}, f32[7,128]{1,0:T(8,128)S(1)}, u32[]{:S(2)}, u32[]{:S(2)}) collective-permute-start(f32[7,128]{1,0:T(8,128)S(1)} %get-tuple-element.31), channel_id=1, source_target_pairs={{0,32},{32,64},{64,96},{96,128},{128,160},{160,192},{192,224},{224... | collective-permute-start | bytes 10760 | tf_op jit(solution)/shard_map/ppermute | solution.py:29
  236.0 5.5 %collective-permute-start.8 = (f32[7,128]{1,0:T(8,128)S(1)}, f32[7,128]{1,0:T(8,128)S(1)}, u32[]{:S(2)}, u32[]{:S(2)}) collective-permute-start(f32[7,128]{1,0:T(8,128)S(1)} %get-tuple-element.30), channel_id=1, source_target_pairs={{0,24},{8,0},{16,8},{24,16},{1,25},{9,1},{17,9},{25,17},{2,26},{10... | collective-permute-start | bytes 10760 | tf_op jit(solution)/shard_map/ppermute | solution.py:28
  238.9 4.8 %collective-permute-start.9 = (f32[7,128]{1,0:T(8,128)S(1)}, f32[7,128]{1,0:T(8,128)S(1)}, u32[]{:S(2)}, u32[]{:S(2)}) collective-permute-start(f32[7,128]{1,0:T(8,128)S(1)} %get-tuple-element.29), channel_id=1, source_target_pairs={{0,8},{8,16},{16,24},{24,0},{1,9},{9,17},{17,25},{25,1},{2,10},{10... | collective-permute-start | bytes 10760 | tf_op jit(solution)/shard_map/ppermute | solution.py:29
  238.9 4.8 %collective-permute-start.10 = (f32[7,256]{1,0:T(8,128)S(1)}, f32[7,256]{1,0:T(8,128)S(1)}, u32[]{:S(2)}, u32[]{:S(2)}) collective-permute-start(f32[7,256]{1,0:T(8,128)S(1)} %get-tuple-element.28), channel_id=1, source_target_pairs={{0,7},{1,0},{2,1},{3,2},{4,3},{5,4},{6,5},{7,6},{8,15},{9,8},{10,9... | collective-permute-start | bytes 21512 | tf_op jit(solution)/shard_map/ppermute | solution.py:28
  241.1 3.7 %collective-permute-start.11 = (f32[7,256]{1,0:T(8,128)S(1)}, f32[7,256]{1,0:T(8,128)S(1)}, u32[]{:S(2)}, u32[]{:S(2)}) collective-permute-start(f32[7,256]{1,0:T(8,128)S(1)} %get-tuple-element.27), channel_id=1, source_target_pairs={{0,1},{1,2},{2,3},{3,4},{4,5},{5,6},{6,7},{7,0},{8,9},{9,10},{10,1... | collective-permute-start | bytes 21512 | tf_op jit(solution)/shard_map/ppermute | solution.py:29
  244.8 35.4 %copy-start = (f32[7,1024]{1,0:T(8,128)}, f32[7,1024]{1,0:T(8,128)S(1)}, u32[]{:S(2)}) copy-start(f32[7,1024]{1,0:T(8,128)S(1)} %get-tuple-element.14.w_ref) | copy-start | bytes 86020
  247.2 17.1 %collective-permute-start.12 = (f32[7,128]{1,0:T(8,128)S(1)}, f32[7,128]{1,0:T(8,128)S(1)}, u32[]{:S(2)}, u32[]{:S(2)}) collective-permute-start(f32[7,128]{1,0:T(8,128)S(1)} %get-tuple-element.26), channel_id=1, source_target_pairs={{0,224},{32,0},{64,32},{96,64},{128,96},{160,128},{192,160},{224,1... | collective-permute-start | bytes 10760 | tf_op jit(solution)/shard_map/ppermute | solution.py:28
  249.2 21.5 %all-to-all-start.2 = ((f32[32,8,128]{2,1,0:T(8,128)}), f32[32,8,128]{2,1,0:T(8,128)S(1)}, u32[]{:S(2)}, u32[]{:S(2)}) async-start(f32[32,8,128]{2,1,0:T(8,128)} %broadcast_in_dim.62), calls=%async_computation.2 | async-start | bytes 262144 | tf_op jit(solution)/shard_map/all_to_all | solution.py:74
  260.9 4.9 %collective-permute-start.13 = (f32[7,128]{1,0:T(8,128)S(1)}, f32[7,128]{1,0:T(8,128)S(1)}, u32[]{:S(2)}, u32[]{:S(2)}) collective-permute-start(f32[7,128]{1,0:T(8,128)S(1)} %get-tuple-element.25), channel_id=1, source_target_pairs={{0,32},{32,64},{64,96},{96,128},{128,160},{160,192},{192,224},{224... | collective-permute-start | bytes 10760 | tf_op jit(solution)/shard_map/ppermute | solution.py:29
  260.9 4.8 %collective-permute-start.14 = (f32[7,128]{1,0:T(8,128)S(1)}, f32[7,128]{1,0:T(8,128)S(1)}, u32[]{:S(2)}, u32[]{:S(2)}) collective-permute-start(f32[7,128]{1,0:T(8,128)S(1)} %get-tuple-element.24), channel_id=1, source_target_pairs={{0,24},{8,0},{16,8},{24,16},{1,25},{9,1},{17,9},{25,17},{2,26},{10... | collective-permute-start | bytes 10760 | tf_op jit(solution)/shard_map/ppermute | solution.py:28
  263.8 4.9 %collective-permute-start.15 = (f32[7,128]{1,0:T(8,128)S(1)}, f32[7,128]{1,0:T(8,128)S(1)}, u32[]{:S(2)}, u32[]{:S(2)}) collective-permute-start(f32[7,128]{1,0:T(8,128)S(1)} %get-tuple-element.23), channel_id=1, source_target_pairs={{0,8},{8,16},{16,24},{24,0},{1,9},{9,17},{17,25},{25,1},{2,10},{10... | collective-permute-start | bytes 10760 | tf_op jit(solution)/shard_map/ppermute | solution.py:29
  263.8 4.9 %collective-permute-start.16 = (f32[7,256]{1,0:T(8,128)S(1)}, f32[7,256]{1,0:T(8,128)S(1)}, u32[]{:S(2)}, u32[]{:S(2)}) collective-permute-start(f32[7,256]{1,0:T(8,128)S(1)} %get-tuple-element.22), channel_id=1, source_target_pairs={{0,7},{1,0},{2,1},{3,2},{4,3},{5,4},{6,5},{7,6},{8,15},{9,8},{10,9... | collective-permute-start | bytes 21512 | tf_op jit(solution)/shard_map/ppermute | solution.py:28
  264.3 10.4 %collective-permute-start.17 = (f32[7,256]{1,0:T(8,128)S(1)}, f32[7,256]{1,0:T(8,128)S(1)}, u32[]{:S(2)}, u32[]{:S(2)}) collective-permute-start(f32[7,256]{1,0:T(8,128)S(1)} %get-tuple-element.21), channel_id=1, source_target_pairs={{0,1},{1,2},{2,3},{3,4},{4,5},{5,6},{6,7},{7,0},{8,9},{9,10},{10,1... | collective-permute-start | bytes 21512 | tf_op jit(solution)/shard_map/ppermute | solution.py:29
  271.4 8.7 %all-to-all-start.3 = ((f32[8,8,128]{2,1,0:T(8,128)}), f32[8,8,128]{2,1,0:T(8,128)S(1)}, u32[]{:S(2)}, u32[]{:S(2)}) async-start(f32[8,8,128]{2,1,0:T(8,128)} %broadcast_in_dim.63), calls=%async_computation.3 | async-start | bytes 65536 | tf_op jit(solution)/shard_map/all_to_all | solution.py:171
  280.1 0.6 copy-start.2
